TPU v7x, 128 devices: a whole 4x4x4 slice. The times are simulated.
128 devices in a mesh: fac: 32 (over y, x, z_hi), loc: 4 (over z_lo, core).
Axes of the slice: x: 4, y: 4, z: 4 (z_hi: 2, z_lo: 2; z = z_hi * 2 + z_lo), core: 2. Of those that a mesh axis runs over, the one named last changes fastest.
Arguments:
- quad_cost: float32 [128, 128, 128, 128], P('fac', 'loc'), may hold values from -30 to 30
- leader: float32 [128, 128], P('fac', 'loc'), may hold values from -4 to 4
Outputs:
- new_cost: float32 [128, 128, 128, 128], P('fac', 'loc')
- new_leader: float32 [128, 128], P('fac', 'loc')
All inputs are finite; a program needn't handle non-finite values.
Results may differ from a plain program's by a relative error of at most 0.0001.
Values sent between devices are 32-bit elements; how exact they have to be, the bound alone decides.
No kernel may reach another device: no remote copies, remote signals or barrier semaphores. Data moves between devices by JAX's collectives and lax.ppermute only.
A program may use at most 192 MiB of HBM per device.

v0:
```python
import jax
import jax.numpy as jnp
from jax import lax
from jax.sharding import PartitionSpec as P

N = 128
SWEEPS = 3


temper = 0.15
leader_temper = 0.1


def combined_all(x, axis, combine):
    everything = jax.tree.map(lambda part: lax.all_gather(part, axis), x)
    initial = jax.tree.map(lambda part: part[0], everything)

    def hop(k, so_far):
        return combine(so_far, jax.tree.map(lambda part: part[k], everything))

    return lax.fori_loop(1, lax.axis_size(axis), hop, initial)


def soft_min(values, axis, scale):
    scaled = -values / scale
    highest = jnp.max(scaled, axis=axis, keepdims=True)
    totals = jnp.sum(jnp.exp(scaled - highest), axis=axis, keepdims=True)
    return jnp.squeeze(-scale * (highest + jnp.log(totals)), axis)


def partial_totals(values, axis):
    scaled = -values / leader_temper
    highest = jnp.max(scaled, axis=axis)
    totals = jnp.sum(jnp.exp(scaled - jnp.expand_dims(highest, axis)), axis=axis)
    return (highest, totals)


def join_totals(first, second):
    highest = jnp.maximum(first[0], second[0])
    totals = first[1] * jnp.exp(first[0] - highest) + second[1] * jnp.exp(second[0] - highest)
    return (highest, totals)


def sweep_block(block):
    col_dual = jnp.zeros(block.shape[:-2] + (block.shape[-1],), jnp.float32)
    row_dual = jnp.zeros(block.shape[:-1], jnp.float32)
    for sweep in range(SWEEPS):
        row_dual = soft_min(block - col_dual[..., None, :], -1, temper)
        col_dual = soft_min(block - row_dual[..., :, None], -2, temper)
    reduced = block - row_dual[..., :, None] - col_dual[..., None, :]
    worth = (jnp.sum(row_dual, -1) + jnp.sum(col_dual, -1)) / N
    return (reduced, worth)


def on_device(quad_cost, leader):
    fac_rows = quad_cost.shape[0]
    loc_rows = quad_cost.shape[1]
    fac_count = lax.axis_size("fac")
    loc_count = lax.axis_size("loc")
    reduced, worth = sweep_block(quad_cost)
    outgoing = reduced.reshape(fac_rows, loc_rows, fac_count, fac_rows, loc_count, loc_rows)
    outgoing = outgoing.transpose(2, 4, 3, 5, 0, 1).reshape(
        fac_count, loc_count, fac_rows, loc_rows, fac_rows * loc_rows
    )
    flat_out = outgoing.reshape(fac_count * loc_count, fac_rows, loc_rows, fac_rows * loc_rows)
    incoming = lax.all_to_all(flat_out, ("fac", "loc"), split_axis=0, concat_axis=0, tiled=True)
    partner = incoming.reshape(fac_count, loc_count, fac_rows, loc_rows, fac_rows, loc_rows)
    partner = partner.transpose(2, 3, 0, 4, 1, 5).reshape(fac_rows, loc_rows, N, N)
    quad_cost = 0.5 * (reduced + partner)
    leader = leader + worth
    highest, totals = combined_all(partial_totals(leader, 1), "loc", join_totals)
    leader = leader - (-leader_temper * (highest + jnp.log(totals)))[:, None]
    highest, totals = combined_all(partial_totals(leader, 0), "fac", join_totals)
    leader = leader - (-leader_temper * (highest + jnp.log(totals)))[None, :]
    return (quad_cost, leader)


def solution(mesh):
    return jax.shard_map(
        on_device,
        mesh=mesh,
        in_specs=(P("fac", "loc", None, None), P("fac", "loc")),
        out_specs=(P("fac", "loc", None, None), P("fac", "loc")),
        check_vma=False,
    )
```

profile of v0, /device:TPU:96, one launch (start us, length us, event | category | flops | bytes accessed | tf_op | source)
XLA Modules:
  0.0 440.5 jit_solution(12565913801845653264)
XLA Ops:
  0.6 5.8 %fusion.4 = f32[4,32,128]{2,1,0:T(8,128)S(1)} fusion(f32[4,32,128,128]{3,2,1,0:T(8,128)} %param.6), kind=kLoop, calls=%fused_computation.26 | loop fusion | flops 6275072 | bytes 8454144 | tf_op jit(solution)/shard_map/reduce_max | solution.py:26
  6.4 4.8 %exponential_reduce_fusion.5 = f32[4,32,128]{2,1,0:T(8,128)S(1)} fusion(f32[4,32,128,128]{3,2,1,0:T(8,128)S(1)} %copy-done, f32[4,32,128]{2,1,0:T(8,128)S(1)} %fusion.4), kind=kLoop, calls=%fused_computation.23 | loop fusion | flops 8372224 | bytes 8519680 | tf_op jit(solution)/shard_map/reduce_sum | solution.py:27
  11.3 2.6 fusion.5
  13.9 2.8 exponential_reduce_fusion.4
  16.7 2.2 fusion.6
  18.9 4.8 %exponential_reduce_fusion.3 = f32[4,32,128]{2,1,0:T(8,128)S(1)} fusion(f32[4,32,128,128]{3,2,1,0:T(8,128)S(1)} %copy-done, f32[4,32,128]{2,1,0:T(8,128)S(1)} %fusion.6, f32[4,32,128]{2,1,0:T(8,128)S(1)} %add_multiply_fusion.5), kind=kLoop, calls=%fused_computation.19 | loop fusion | flops 10469376 | bytes 8585216 | tf_op jit(solution)/shard_map/reduce_sum | solution.py:27
  23.8 2.6 fusion.7
  26.4 2.8 exponential_reduce_fusion.2
  29.2 2.2 fusion.8
  31.4 4.8 %exponential_reduce_fusion.1 = f32[4,32,128]{2,1,0:T(8,128)S(1)} fusion(f32[4,32,128,128]{3,2,1,0:T(8,128)S(1)} %copy-done, f32[4,32,128]{2,1,0:T(8,128)S(1)} %fusion.8, f32[4,32,128]{2,1,0:T(8,128)S(1)} %add_multiply_fusion.3), kind=kLoop, calls=%fused_computation.15 | loop fusion | flops 10469376 | bytes 8585216 | tf_op jit(solution)/shard_map/reduce_sum | solution.py:27
  36.4 2.6 fusion.9
  39.0 3.0 exponential_reduce_fusion
  42.1 4.6 %subtract_subtract_fusion = f32[4,32,128,128]{3,2,1,0:T(8,128)} fusion(f32[4,32,128,128]{3,2,1,0:T(8,128)S(1)} %copy-done, f32[4,32,128]{2,1,0:T(8,128)S(1)} %get-tuple-element.303, f32[4,32,128]{2,1,0:T(8,128)S(1)} %get-tuple-element.305), kind=kLoop, calls=%fused_computation.25 | loop fusion | flops 4194304 | bytes 16908288 | tf_op jit(solution)/shard_map/sub | solution.py:50
  46.7 23.9 %reshape.83 = f32[4,32,32,4,4,32]{5,4,3,2,1,0:T(4,128)} reshape(f32[4,32,128,128]{3,2,1,0:T(8,128)} %subtract_subtract_fusion) | data formatting | bytes 16777216 | tf_op jit(solution)/shard_map/reshape | solution.py:61
  70.6 44.9 %copy.5 = f32[4,32,32,4,4,32]{1,0,5,3,4,2:T(4,128)} copy(f32[4,32,32,4,4,32]{5,4,3,2,1,0:T(4,128)} %reshape.83) | data formatting | bytes 16777216 | tf_op jit(solution)/shard_map/reshape | solution.py:61
  115.5 25.7 %reshape_reshape.3 = f32[128,4,32,128]{3,2,1,0:T(8,128)} reshape(f32[32,4,4,32,4,32]{5,4,3,2,1,0:T(4,128)} %bitcast.38) | data formatting | bytes 16777216 | tf_op jit(solution)/shard_map/reshape;reshape | solution.py:65
  141.2 10.3 %all-to-all-start = ((f32[128,4,32,128]{3,2,1,0:T(8,128)}), f32[128,4,32,128]{3,2,1,0:T(8,128)}, u32[]{:S(2)}, u32[]{:S(2)}) async-start(f32[128,4,32,128]{3,2,1,0:T(8,128)} %reshape_reshape.3), calls=%async_computation | async-start | bytes 16777216 | tf_op jit(solution)/shard_map/all_to_all | solution.py:66
  154.2 80.2 %all-reduce.5 = (f32[16]{0:T(128)S(1)}, f32[16]{0:T(128)S(1)}) all-reduce(f32[16]{0:T(128)S(1)} %dynamic-update-slice, f32[16]{0:T(128)S(1)} %dynamic-update-slice.1), channel_id=2, replica_groups=mesh['fac'=32,'loc'=4] {'loc'}, use_global_device_ids=true, to_apply=%add | all-reduce | flops 32 | bytes 256
  235.9 104.6 %all-reduce.4 = (f32[1024]{0:T(1024)S(1)}, f32[1024]{0:T(1024)S(1)}) all-reduce(f32[1024]{0:T(1024)S(1)} %dynamic-update-slice.2, f32[1024]{0:T(1024)S(1)} %dynamic-update-slice.3), channel_id=4, replica_groups=mesh['fac'=32,'loc'=4] {'fac'}, use_global_device_ids=true, to_apply=%add.2 | all-reduce | flops 2048 | bytes 16384
  340.7 1.5 while.35
  342.9 23.9 %reshape.84 = f32[32,4,4,32,4,32]{5,4,3,2,1,0:T(4,128)} reshape(f32[128,4,32,128]{3,2,1,0:T(8,128)} %all-to-all-done) | data formatting | bytes 16777216 | tf_op jit(solution)/shard_map/reshape | solution.py:67
  366.8 38.0 %copy.6 = f32[4,32,32,4,4,32]{5,4,3,2,1,0:T(4,128)} copy(f32[4,32,32,4,4,32]{5,3,1,0,4,2:T(4,128)} %bitcast.39) | data formatting | bytes 16777216 | tf_op jit(solution)/shard_map/transpose | solution.py:68
  404.8 25.7 %reshape.85 = f32[4,32,128,128]{3,2,1,0:T(8,128)} reshape(f32[4,32,32,4,4,32]{5,4,3,2,1,0:T(4,128)} %copy.6) | data formatting | bytes 16777216 | tf_op jit(solution)/shard_map/reshape | solution.py:68
  430.5 10.0 %add_multiply_fusion = f32[4,32,128,128]{3,2,1,0:T(8,128)} fusion(f32[4,32,128,128]{3,2,1,0:T(8,128)} %reshape.85, f32[4,32,128]{2,1,0:T(8,128)S(1)} %get-tuple-element.303, f32[4,32,128,128]{3,2,1,0:T(8,128)} %param.6, f32[4,32,128]{2,1,0:T(8,128)S(1)} %get-tuple-element.305), kind=kLoop, calls=%fused_computation.12 | loop fusion | flops 8388608 | bytes 25296896 | tf_op jit(solution)/shard_map/mul | solution.py:69
  (73 shorter events, 5.0 us)
Async XLA Ops:
  0.6 5.8 %copy-start = (f32[4,32,128,128]{3,2,1,0:T(8,128)S(1)}, f32[4,32,128,128]{3,2,1,0:T(8,128)}, u32[]{:S(2)}) copy-start(f32[4,32,128,128]{3,2,1,0:T(8,128)} %param.6) | copy-start | bytes 25165828
  141.2 10.3 %copy-start.3 = (u32[128]{0:T(128)S(1)}, u32[128]{0:T(128)}, u32[]{:S(2)}) copy-start(u32[128]{0:T(128)} %constant.114) | copy-start | bytes 1540
  141.2 10.9 %copy-start.2 = (u32[128]{0:T(128)S(1)}, u32[128]{0:T(128)}, u32[]{:S(2)}) copy-start(u32[128]{0:T(128)} %constant.104) | copy-start | bytes 1540
  141.2 12.2 %copy-start.1 = (f32[4,32]{1,0:T(4,128)S(1)}, f32[4,32]{1,0:T(4,128)}, u32[]{:S(2)}) copy-start(f32[4,32]{1,0:T(4,128)} %param.7) | copy-start | bytes 1540
  141.2 201.7 %all-to-all-start = ((f32[128,4,32,128]{3,2,1,0:T(8,128)}), f32[128,4,32,128]{3,2,1,0:T(8,128)}, u32[]{:S(2)}, u32[]{:S(2)}) async-start(f32[128,4,32,128]{3,2,1,0:T(8,128)} %reshape_reshape.3), calls=%async_computation | async-start | bytes 16777216 | tf_op jit(solution)/shard_map/all_to_all | solution.py:66
where the time goes:
time: 444 us; the launch traced here: 441 us
  local copies, waits for them, and re-layouts  185 us (42%)
  blocking collectives  185 us (42%)
  other arithmetic  58 us (13%)
  starting transfers between devices  10.3 us (2%)
    unnamed x2, blocking collectives  185 us
    reshape x2, local copies, waits for them, and re-layouts, on_device(): reduced.reshape(fac_rows, loc_rows, fac_count, fac_rows, loc_count, loc_r...  68.8 us
    transpose x1, local copies, waits for them, and re-layouts, on_device(): partner.transpose(2, 3, 0, 4, 1, 5).reshape(fac_rows, loc_rows, N, N)  38 us
    reshape x1, local copies, waits for them, and re-layouts, on_device(): partner.transpose(2, 3, 0, 4, 1, 5).reshape(fac_rows, loc_rows, N, N)  25.7 us
    another operation x1, local copies, waits for them, and re-layouts, on_device(): outgoing.reshape(fac_count * loc_count, fac_rows, loc_rows, fac_rows * lo...  25.7 us
    reshape x1, local copies, waits for them, and re-layouts, on_device(): incoming.reshape(fac_count, loc_count, fac_rows, loc_rows, fac_rows, loc_...  23.9 us
    reduce_sum x6, other arithmetic, soft_min(): totals = jnp.sum(jnp.exp(scaled - highest), axis=axis, keepdims=True)  22.9 us
    reduce_max x6, other arithmetic, soft_min(): highest = jnp.max(scaled, axis=axis, keepdims=True)  18.1 us
  transfers between devices with their start and end apart: 1, of which 0 were waited for; matrix products, arithmetic and copies ran while one was open for 1% of the time, Pallas kernels for 0%

commit v1 on v0

v1 whole, which is shorter than its diff:
```python
import jax
import jax.numpy as jnp
from jax import lax
from jax.experimental import pallas as pl
from jax.experimental.pallas import tpu as pltpu
from jax.sharding import PartitionSpec as P

N = 128
FAC = 32
LOC = 4
FR = N // FAC
LR = N // LOC

temper = 0.15
leader_temper = 0.1
LOG2E = 1.4426950408889634
INNER = LOG2E / temper
UNROLL = 2


def over_groups(x, combine):
    x = combine(x, pltpu.roll(x, LR, 1))
    return combine(x, pltpu.roll(x, 2 * LR, 1))


def sweep_kernel(c_ref, s_ref, u_ref, v_ref, w_ref, d_ref, e_ref, m_ref, a_ref):
    def load(f, col_min):
        rows = [c_ref[pl.ds(FR * f + k, LR, stride=N), :] for k in range(FR)]
        x = jnp.concatenate(rows, 0).T
        row_min = jnp.min(x, 0, keepdims=True)
        x = x - row_min
        d_ref[f] = x
        m_ref[pl.ds(f, 1), :] = row_min
        return jnp.minimum(col_min, x)

    col_min = lax.fori_loop(0, FAC, load, jnp.full((N, N), jnp.inf, jnp.float32), unroll=UNROLL)
    col_min = over_groups(col_min, jnp.minimum)

    weight = jnp.exp2(-INNER * col_min)

    def first(f, total):
        e = jnp.exp2(INNER * (col_min - d_ref[f]))
        e_ref[f] = e
        a = 1.0 / jnp.sum(e * weight, 0, keepdims=True)
        return total + e * a

    zero = jnp.zeros((N, N), jnp.float32)
    b = 1.0 / over_groups(lax.fori_loop(0, FAC, first, zero, unroll=UNROLL), jnp.add)

    for _ in range(2):

        def later(f, total, b=b):
            e = e_ref[f]
            a = 1.0 / jnp.sum(e * b, 0, keepdims=True)
            a_ref[pl.ds(f, 1), :] = a
            return total + e * a

        b = 1.0 / over_groups(lax.fori_loop(0, FAC, later, zero, unroll=UNROLL), jnp.add)

    row_part = temper * jnp.log(a_ref[...])
    a_ref[...] = row_part
    col = col_min + temper * jnp.log(b)

    def emit(f, carry):
        r = d_ref[f] - col - a_ref[pl.ds(f, 1), :]
        s_ref[pl.ds(f * LOC, LOC), :, :] = r.reshape(LOC, LR, N)
        return carry

    lax.fori_loop(0, FAC, emit, 0, unroll=UNROLL)
    row = m_ref[...] + row_part
    u_ref[...] = jnp.concatenate([row, jnp.zeros((N - FAC, N), jnp.float32)], 0).T
    v_ref[...] = col.T[:LR]
    worth = over_groups(jnp.sum(row, 0, keepdims=True), jnp.add) + jnp.sum(col, 0, keepdims=True)
    w_ref[...] = worth * (1.0 / N)


def sweeps(quad_cost):
    rows = LR * N
    return pl.pallas_call(
        sweep_kernel,
        grid=(FR,),
        in_specs=[pl.BlockSpec((rows, N), lambda i: (i, 0))],
        out_specs=[
            pl.BlockSpec((FAC * LOC, None, LR, N), lambda i: (0, i, 0, 0)),
            pl.BlockSpec((None, N, N), lambda i: (i, 0, 0)),
            pl.BlockSpec((None, LR, N), lambda i: (i, 0, 0)),
            pl.BlockSpec((None, 1, N), lambda i: (i, 0, 0)),
        ],
        out_shape=[
            jax.ShapeDtypeStruct((FAC * LOC, FR, LR, N), jnp.float32),
            jax.ShapeDtypeStruct((FR, N, N), jnp.float32),
            jax.ShapeDtypeStruct((FR, LR, N), jnp.float32),
            jax.ShapeDtypeStruct((FR, 1, N), jnp.float32),
        ],
        scratch_shapes=[
            pltpu.VMEM((FAC, N, N), jnp.float32),
            pltpu.VMEM((FAC, N, N), jnp.float32),
            pltpu.VMEM((FAC, N), jnp.float32),
            pltpu.VMEM((FAC, N), jnp.float32),
        ],
    )(quad_cost.reshape(FR * rows, N))


def regroup(parts):
    lane = lax.broadcasted_iota(jnp.int32, parts[0].shape, 1)
    low = lane < 2 * LR
    p0, p1, p2, p3 = parts
    q0 = jnp.where(low, p0, pltpu.roll(p2, 2 * LR, 1))
    q2 = jnp.where(low, pltpu.roll(p0, 2 * LR, 1), p2)
    q1 = jnp.where(low, p1, pltpu.roll(p3, 2 * LR, 1))
    q3 = jnp.where(low, pltpu.roll(p1, 2 * LR, 1), p3)
    even = (lane & LR) == 0
    return [
        jnp.where(even, q0, pltpu.roll(q1, LR, 1)),
        jnp.where(even, pltpu.roll(q0, 3 * LR, 1), q1),
        jnp.where(even, q2, pltpu.roll(q3, LR, 1)),
        jnp.where(even, pltpu.roll(q2, 3 * LR, 1), q3),
    ]


STEP = 8
STEP_F = STEP // FR


def soft_min(values, axis, scale):
    scaled = -values / scale
    highest = jnp.max(scaled, axis=axis, keepdims=True)
    totals = jnp.sum(jnp.exp(scaled - highest), axis=axis, keepdims=True)
    return -scale * (highest + jnp.log(totals))


def join_kernel(place_ref, c_ref, r_ref, u_ref, v_ref, b_ref, o_ref, nb_ref, bs_ref):
    step = pl.program_id(0)
    c_rows = c_ref.reshape(FR * LR * STEP, N)
    o_rows = o_ref.reshape(FR * LR * STEP, N)

    @pl.when(step == 0)
    def _():
        b = regroup([b_ref[pl.ds(g, FAC, stride=LOC), :] for g in range(LOC)])
        b = [x - soft_min(x, 1, leader_temper) for x in b]
        b = jnp.concatenate(b, 0)
        bs_ref[...] = b - soft_min(b, 0, leader_temper)
        for i in range(FR):
            row = bs_ref[pl.ds(i * FAC + place_ref[0], 1), :]
            row = pltpu.roll(row, (LOC - place_ref[1]) * LR, 1)
            nb_ref[pl.ds(i, 1), :] = row[:, :LR]

    for g in range(STEP_F):
        f = step * STEP_F + g
        shift = lax.rem(N - f, N)
        for k in range(FR):
            for t in range(LR // 8):
                parts = [r_ref[g * LOC + s, k, pl.ds(t * 8, 8), :] for s in range(LOC)]
                parts = regroup(parts)
                for a in range(FR):
                    at = pl.ds((a * LR + t * 8) * STEP + g * FR + k, 8, stride=STEP)
                    row = u_ref[a, pl.ds(k * LR + t * 8, 8), :]
                    row = pltpu.roll(row, shift, 1)[:, :1]
                    own = c_rows[at, :] - row - v_ref[a, pl.ds(t * 8, 8), :]
                    o_rows[at, :] = 0.5 * (own + parts[a])


def join(quad_cost, incoming, row, col, leader, place):
    return pl.pallas_call(
        join_kernel,
        grid_spec=pltpu.PrefetchScalarGridSpec(
            num_scalar_prefetch=1,
            grid=(N // STEP,),
            in_specs=[
                pl.BlockSpec((FR, LR, STEP, N), lambda i, p: (0, 0, i, 0)),
                pl.BlockSpec((STEP_F * LOC, FR, LR, N), lambda i, p: (i, 0, 0, 0)),
                pl.BlockSpec((FR, N, N), lambda i, p: (0, 0, 0)),
                pl.BlockSpec((FR, LR, N), lambda i, p: (0, 0, 0)),
                pl.BlockSpec((N, N), lambda i, p: (0, 0)),
            ],
            out_specs=[
                pl.BlockSpec((FR, LR, STEP, N), lambda i, p: (0, 0, i, 0)),
                pl.BlockSpec((FR, LR), lambda i, p: (0, 0)),
            ],
            scratch_shapes=[pltpu.VMEM((N, N), jnp.float32)],
        ),
        out_shape=[
            jax.ShapeDtypeStruct((FR, LR, N, N), jnp.float32),
            jax.ShapeDtypeStruct((FR, LR), jnp.float32),
        ],
    )(place, quad_cost, incoming, row, col, leader)


def on_device(quad_cost, leader):
    send, row, col, worth = sweeps(quad_cost)
    leader = leader + worth[:, 0, :LR]
    incoming = lax.all_to_all(send, ("fac", "loc"), split_axis=0, concat_axis=0, tiled=True)
    everywhere = lax.all_gather(leader.reshape(1, N), ("fac", "loc"), tiled=True)
    place = jnp.stack([lax.axis_index("fac"), lax.axis_index("loc")]).astype(jnp.int32)
    quad_cost, leader = join(quad_cost, incoming, row, col, everywhere, place)
    return quad_cost, leader


def solution(mesh):
    return jax.shard_map(
        on_device,
        mesh=mesh,
        in_specs=(P("fac", "loc", None, None), P("fac", "loc")),
        out_specs=(P("fac", "loc", None, None), P("fac", "loc")),
        check_vma=False,
    )
```

time: 444 us -> 237 us (0.53)
  the two profiles are of different devices: /device:TPU:96 before, /device:TPU:3 now
where the time goes in v1:
time: 237 us; the launch traced here: 236 us
  blocking collectives  130 us (55%)
  Pallas kernels  94 us (40%)
  starting transfers between devices  11.3 us (5%)
    all_gather x1, blocking collectives, on_device(): lax.all_gather(leader.reshape(1, N), ('fac', 'loc'), tiled=True)  130 us
    pallas_call x1, Pallas kernels, join(): pl.pallas_call(join_kernel, grid_spec=pltpu.PrefetchScalarGridSpec(num_sc...  67.3 us
    pallas_call x1, Pallas kernels, sweeps(): pl.pallas_call(sweep_kernel, grid=(FR,), in_specs=[pl.BlockSpec((rows, N)...  26.7 us
    all_to_all x1, starting transfers between devices, on_device(): lax.all_to_all(send, ('fac', 'loc'), split_axis=0, concat_axis=0, tiled=T...  11.3 us
  transfers between devices with their start and end apart: 1, of which 0 were waited for; matrix products, arithmetic and copies ran while one was open for 0% of the time, Pallas kernels for 0%

profile of v1, /device:TPU:3, one launch (start us, length us, event | category | flops | bytes accessed | tf_op | source)
XLA Modules:
  0.0 236.3 jit_solution(8042852765142886807)
XLA Ops:
  0.6 26.7 %shard_map.41 = (f32[128,4,32,128]{3,2,1,0:T(8,128)}, f32[4,128,128]{2,1,0:T(8,128)}, f32[4,32,128]{2,1,0:T(8,128)}, f32[4,1,128]{2,1,0:T(1,128)}) custom-call(f32[16384,128]{1,0:T(8,128)} %bitcast.6), custom_call_target="tpu_custom_call" | custom-call | tf_op jit(solution)/shard_map/pallas_call | solution.py:79
  27.3 0.0 copy-start
  27.3 0.0 copy-start.1
  27.4 11.3 %all-to-all-start = ((f32[128,4,32,128]{3,2,1,0:T(8,128)}), f32[128,4,32,128]{3,2,1,0:T(8,128)}, u32[]{:S(2)}, u32[]{:S(2)}) async-start(f32[128,4,32,128]{3,2,1,0:T(8,128)} %get-tuple-element.6), calls=%async_computation | async-start | bytes 16777216 | tf_op jit(solution)/shard_map/all_to_all | solution.py:192
  38.6 0.0 copy-done
  38.7 0.0 copy-done.1
  38.7 0.1 reshape.12
  38.8 129.6 %all-gather = f32[128,1,128]{2,1,0:T(1,128)} all-gather(f32[1,1,128]{2,1,0:T(1,128)S(1)} %reshape.12), channel_id=1, replica_groups=mesh['fac'=32,'loc'=4] {'fac','loc'}, dimensions={0}, use_global_device_ids=true | all-gather | bytes 66048 | tf_op jit(solution)/shard_map/all_gather | solution.py:193
  168.4 0.6 pad_add_fusion.place_ref
  169.0 0.0 all-to-all-done.r_ref
  169.0 67.3 %shard_map.42 = (f32[4,32,128,128]{3,2,1,0:T(8,128)}, f32[4,32]{1,0:T(4,128)}) custom-call(s32[2]{0:T(128)} %pad_add_fusion.place_ref, f32[4,32,128,128]{3,2,1,0:T(8,128)} %c_ref.1, f32[128,4,32,128]{3,2,1,0:T(8,128)} %all-to-all-done.r_ref, f32[4,128,128]{2,1,0:T(8,128)} %get-tuple-element.7.u_ref, f32[4,32,128]{2,1,0:T(8,128)} %get-tuple-element.8.v_ref, ...), custom_call_target="tpu_custom_call" | custom-call | tf_op jit(solution)/shard_map/pallas_call | solution.py:164
  (1 shorter events, 0.0 us)
Async XLA Ops:
  27.3 11.3 %copy-start = (f32[4,32]{1,0:T(4,128)S(1)}, f32[4,32]{1,0:T(4,128)}, u32[]{:S(2)}) copy-start(f32[4,32]{1,0:T(4,128)} %param.3) | copy-start | bytes 1540
  27.3 11.3 %copy-start.1 = (f32[4,1,128]{2,1,0:T(1,128)S(1)}, f32[4,1,128]{2,1,0:T(1,128)}, u32[]{:S(2)}) copy-start(f32[4,1,128]{2,1,0:T(1,128)} %get-tuple-element.9) | copy-start | bytes 6148
  27.4 141.6 %all-to-all-start = ((f32[128,4,32,128]{3,2,1,0:T(8,128)}), f32[128,4,32,128]{3,2,1,0:T(8,128)}, u32[]{:S(2)}, u32[]{:S(2)}) async-start(f32[128,4,32,128]{3,2,1,0:T(8,128)} %get-tuple-element.6), calls=%async_computation | async-start | bytes 16777216 | tf_op jit(solution)/shard_map/all_to_all | solution.py:192

commit v2 on v1

v2 whole, which is shorter than its diff:
```python
import jax
import jax.numpy as jnp
from jax import lax
from jax.experimental import pallas as pl
from jax.experimental.pallas import tpu as pltpu
from jax.sharding import PartitionSpec as P

N = 128
FAC = 32
LOC = 4
FR = N // FAC
LR = N // LOC

temper = 0.15
leader_temper = 0.1
LOG2E = 1.4426950408889634
INNER = LOG2E / temper
UNROLL = 8
DEVICES = FAC * LOC
PIECE = N + 1
STEP = 16
STEP_F = STEP // FR
VMEM_LIMIT = 60 << 20
AXES = ("fac", "loc")


def over_groups(x, combine):
    x = combine(x, pltpu.roll(x, LR, 1))
    return combine(x, pltpu.roll(x, 2 * LR, 1))


def sweep_kernel(c_ref, b_ref, s_ref, u_ref, v_ref, d_ref, e_ref, m_ref, a_ref, w_ref, out_ref, line_ref, sem, line_sem):
    slab = pl.program_id(0)
    slot = slab & 1
    loc = lax.axis_index("loc")

    def load(f, col_min):
        rows = []
        for g in range(LOC):
            k = (g + LOC - loc) & (LOC - 1)
            rows.append(c_ref[pl.ds(FR * f + k, LR, stride=N), :])
        x = jnp.concatenate(rows, 0).T
        row_min = jnp.min(x, 0, keepdims=True)
        x = x - row_min
        d_ref[f] = x
        m_ref[pl.ds(f, 1), :] = row_min
        return jnp.minimum(col_min, x)

    col_min = lax.fori_loop(0, FAC, load, jnp.full((N, N), jnp.inf, jnp.float32), unroll=UNROLL)
    col_min = over_groups(col_min, jnp.minimum)

    weight = jnp.exp2(-INNER * col_min)

    def first(f, total):
        e = jnp.exp2(INNER * (col_min - d_ref[f]))
        e_ref[f] = e
        a = 1.0 / jnp.sum(e * weight, 0, keepdims=True)
        return total + e * a

    zero = jnp.zeros((N, N), jnp.float32)
    b = 1.0 / over_groups(lax.fori_loop(0, FAC, first, zero, unroll=UNROLL), jnp.add)

    for _ in range(2):

        def later(f, total, b=b):
            e = e_ref[f]
            a = 1.0 / jnp.sum(e * b, 0, keepdims=True)
            a_ref[pl.ds(f, 1), :] = a
            return total + e * a

        b = 1.0 / over_groups(lax.fori_loop(0, FAC, later, zero, unroll=UNROLL), jnp.add)

    row_part = temper * jnp.log(a_ref[...])
    a_ref[...] = row_part
    col = col_min + temper * jnp.log(b)

    def slab_done(at):
        pltpu.make_async_copy(out_ref.at[at], s_ref.at[pl.ds(0, FAC * N)], sem.at[at]).wait()

    @pl.when(slab >= 2)
    def _():
        slab_done(slot)

    def ship(f):
        for s in range(LOC):
            pltpu.make_async_copy(
                out_ref.at[slot, pl.ds(f * N + s * LR, LR)],
                s_ref.at[pl.ds((f * LOC + s) * PIECE + slab * LR, LR)],
                sem.at[slot],
            ).start()

    def emit(f, carry):
        out_ref[slot, pl.ds(pl.multiple_of(f * N, N), N), :] = d_ref[f] - col - a_ref[pl.ds(f, 1), :]

        @pl.when(f > 0)
        def _():
            ship(f - 1)

        return carry

    lax.fori_loop(0, FAC, emit, 0, unroll=UNROLL)
    ship(FAC - 1)
    row = m_ref[...] + row_part
    u_ref[...] = jnp.concatenate([row, jnp.zeros((N - FAC, N), jnp.float32)], 0).T
    v_ref[...] = col.T[:LR]
    worth = over_groups(jnp.sum(row, 0, keepdims=True), jnp.add) + jnp.sum(col, 0, keepdims=True)
    w_ref[pl.ds(slab, 1), :] = worth * (1.0 / N)

    @pl.when(slab == FR - 1)
    def _():
        leader = jnp.concatenate([b_ref[...]] * LOC, 1) + w_ref[...]
        group = lax.broadcasted_iota(jnp.int32, (1, N), 1) // LR
        line = leader[:1]
        for i in range(FR):
            line = jnp.where(group == ((i + loc) & (LOC - 1)), leader[i : i + 1], line)
        line_ref[...] = line

        def send(d, carry):
            pltpu.make_async_copy(line_ref, s_ref.at[pl.ds(d * PIECE + N, 1)], line_sem).start()
            return carry

        lax.fori_loop(0, DEVICES, send, 0, unroll=8)

        pltpu.make_async_copy(out_ref.at[0, pl.ds(0, DEVICES)], s_ref.at[pl.ds(0, DEVICES)], line_sem).wait()
        slab_done(1 - slot)
        slab_done(slot)


def sweeps(quad_cost, leader):
    rows = LR * N
    return pl.pallas_call(
        sweep_kernel,
        grid=(FR,),
        in_specs=[
            pl.BlockSpec((rows, N), lambda i: (i, 0)),
            pl.BlockSpec((FR, LR), lambda i: (0, 0)),
        ],
        out_specs=[
            pl.BlockSpec(memory_space=pl.ANY),
            pl.BlockSpec((None, N, N), lambda i: (i, 0, 0)),
            pl.BlockSpec((None, LR, N), lambda i: (i, 0, 0)),
        ],
        out_shape=[
            jax.ShapeDtypeStruct((DEVICES * PIECE, N), jnp.float32),
            jax.ShapeDtypeStruct((FR, N, N), jnp.float32),
            jax.ShapeDtypeStruct((FR, LR, N), jnp.float32),
        ],
        scratch_shapes=[
            pltpu.VMEM((FAC, N, N), jnp.float32),
            pltpu.VMEM((FAC, N, N), jnp.float32),
            pltpu.VMEM((FAC, N), jnp.float32),
            pltpu.VMEM((FAC, N), jnp.float32),
            pltpu.VMEM((FR, N), jnp.float32),
            pltpu.VMEM((2, FAC * N, N), jnp.float32),
            pltpu.VMEM((1, N), jnp.float32),
            pltpu.SemaphoreType.DMA((2,)),
            pltpu.SemaphoreType.DMA,
        ],
        compiler_params=pltpu.CompilerParams(vmem_limit_bytes=VMEM_LIMIT),
    )(quad_cost.reshape(FR * rows, N), leader)


def own_kernel(c_ref, u_ref, v_ref, o_ref):
    step = pl.program_id(0)
    loc = lax.axis_index("loc")
    c_rows = c_ref.reshape(FR * LR * STEP, N)
    o_rows = o_ref.reshape(FR * LR * STEP, N)
    for g in range(STEP_F):
        shift = lax.rem(N - (step * STEP_F + g), N)
        for k in range(FR):
            begin = ((k + loc) & (FR - 1)) * LR
            for a in range(FR):
                row = u_ref[a, pl.ds(pl.multiple_of(begin, LR), LR), :]
                row = pltpu.roll(row, shift, 1)[:, :1]
                at = pl.ds(a * LR * STEP + g * FR + k, LR, stride=STEP)
                o_rows[at, :] = 0.5 * (c_rows[at, :] - row - v_ref[a])


def own_half(quad_cost, row, col):
    return pl.pallas_call(
        own_kernel,
        grid=(N // STEP,),
        in_specs=[
            pl.BlockSpec((FR, LR, STEP, N), lambda i: (0, 0, i, 0)),
            pl.BlockSpec((FR, N, N), lambda i: (0, 0, 0)),
            pl.BlockSpec((FR, LR, N), lambda i: (0, 0, 0)),
        ],
        out_specs=pl.BlockSpec((FR, LR, STEP, N), lambda i: (0, 0, i, 0)),
        out_shape=jax.ShapeDtypeStruct((FR, LR, N, N), jnp.float32),
        compiler_params=pltpu.CompilerParams(vmem_limit_bytes=VMEM_LIMIT),
        cost_estimate=pl.CostEstimate(flops=1 << 23, bytes_accessed=1 << 24, transcendentals=0),
    )(quad_cost, row, col)


def regroup(parts):
    group = lax.broadcasted_iota(jnp.int32, parts[0].shape, 1) // LR
    odd = (group & 1) == 1
    low = group < 2
    p0, p1, p2, p3 = parts
    even_a, even_b = jnp.where(odd, p1, p0), jnp.where(odd, p3, p2)
    odd_a, odd_b = jnp.where(odd, p0, p3), jnp.where(odd, p2, p1)
    return [
        jnp.where(low, even_a, even_b),
        pltpu.roll(jnp.where(low, odd_a, odd_b), 3 * LR, 1),
        pltpu.roll(jnp.where(low, even_b, even_a), 2 * LR, 1),
        pltpu.roll(jnp.where(low, odd_b, odd_a), LR, 1),
    ]


def soft_min(values, axis, scale):
    scaled = -values / scale
    highest = jnp.max(scaled, axis=axis, keepdims=True)
    totals = jnp.sum(jnp.exp(scaled - highest), axis=axis, keepdims=True)
    return -scale * (highest + jnp.log(totals))


def join_kernel(q_ref, r_ref, o_ref, nb_ref, in_ref, lead_ref, bs_ref, sem, lead_sem):
    step = pl.program_id(0)
    slot = step & 1
    sources = STEP_F * LOC

    def piece(at, n, to):
        return pltpu.make_async_copy(r_ref.at[pl.ds((at * sources + n) * PIECE, N)], in_ref.at[to, n], sem.at[to, n])

    def fetch(at, to):
        for n in range(sources):
            piece(at, n, to).start()

    def lead(d):
        return pltpu.make_async_copy(r_ref.at[pl.ds(d * PIECE + N, 1)], lead_ref.at[pl.ds(d, 1)], lead_sem)

    @pl.when(step == 0)
    def _():
        fetch(0, 0)

        def start(d, carry):
            lead(d).start()
            return carry

        lax.fori_loop(0, DEVICES, start, 0, unroll=8)

    @pl.when(step + 1 < pl.num_programs(0))
    def _():
        fetch(step + 1, 1 - slot)

    @pl.when(step == 1)
    def _():
        pltpu.make_async_copy(r_ref.at[pl.ds(0, DEVICES)], lead_ref, lead_sem).wait()
        fac, loc = (lax.axis_index(name) for name in AXES)
        b = regroup([lead_ref[pl.ds(g, FAC, stride=LOC), :] for g in range(LOC)])
        b = [x - soft_min(x, 1, leader_temper) for x in b]
        b = jnp.concatenate(b, 0)
        bs_ref[...] = b - soft_min(b, 0, leader_temper)
        for i in range(FR):
            row = bs_ref[pl.ds(i * FAC + fac, 1), :]
            row = pltpu.roll(row, (LOC - loc) * LR, 1)
            nb_ref[pl.ds(i, 1), :] = row[:, :LR]

    for n in range(sources):
        piece(step, n, slot).wait()
    q_rows = q_ref.reshape(FR * LR * STEP, N)
    o_rows = o_ref.reshape(FR * LR * STEP, N)
    for g in range(STEP_F):
        for k in range(FR):
            for t in range(LR // 8):
                parts = [in_ref[slot, g * LOC + s, pl.ds(k * LR + t * 8, 8), :] for s in range(LOC)]
                parts = regroup(parts)
                for a in range(FR):
                    at = pl.ds((a * LR + t * 8) * STEP + g * FR + k, 8, stride=STEP)
                    o_rows[at, :] = q_rows[at, :] + 0.5 * parts[a]


def join(own, incoming):
    return pl.pallas_call(
        join_kernel,
        grid=(N // STEP,),
        in_specs=[
            pl.BlockSpec((FR, LR, STEP, N), lambda i: (0, 0, i, 0)),
            pl.BlockSpec(memory_space=pl.ANY),
        ],
        out_specs=[
            pl.BlockSpec((FR, LR, STEP, N), lambda i: (0, 0, i, 0)),
            pl.BlockSpec((FR, LR), lambda i: (0, 0)),
        ],
        out_shape=[
            jax.ShapeDtypeStruct((FR, LR, N, N), jnp.float32),
            jax.ShapeDtypeStruct((FR, LR), jnp.float32),
        ],
        scratch_shapes=[
            pltpu.VMEM((2, STEP_F * LOC, N, N), jnp.float32),
            pltpu.VMEM((DEVICES, N), jnp.float32),
            pltpu.VMEM((N, N), jnp.float32),
            pltpu.SemaphoreType.DMA((2, STEP_F * LOC)),
            pltpu.SemaphoreType.DMA,
        ],
        compiler_params=pltpu.CompilerParams(vmem_limit_bytes=VMEM_LIMIT),
    )(own, incoming)


def on_device(quad_cost, leader):
    send, row, col = sweeps(quad_cost, leader)
    send = send.reshape(DEVICES, PIECE, 1, N)
    incoming = lax.all_to_all(send, AXES, split_axis=0, concat_axis=0, tiled=True)
    own = own_half(quad_cost, row, col)
    return tuple(join(own, incoming.reshape(DEVICES * PIECE, N)))


def solution(mesh):
    return jax.shard_map(
        on_device,
        mesh=mesh,
        in_specs=(P("fac", "loc", None, None), P("fac", "loc")),
        out_specs=(P("fac", "loc", None, None), P("fac", "loc")),
        check_vma=False,
    )
```

time: 237 us -> 150 us (0.63)
  the two profiles are of different devices: /device:TPU:3 before, /device:TPU:53 now
where the time goes in v2:
time: 150 us
  waiting for transfers between devices  72.2 us (48%)
  Pallas kernels  66.3 us (44%)
  starting transfers between devices  10.8 us (7%)
    all_to_all x1, waiting for transfers between devices, on_device(): lax.all_to_all(send, AXES, split_axis=0, concat_axis=0, tiled=True)  72.2 us
    pallas_call x1, Pallas kernels, own_half(): pl.pallas_call(own_kernel, grid=(N // STEP,), in_specs=[pl.BlockSpec((FR,...  33.2 us
    pallas_call x1, Pallas kernels, sweeps(): pl.pallas_call(sweep_kernel, grid=(FR,), in_specs=[pl.BlockSpec((rows, N)...  20.1 us
    pallas_call x1, Pallas kernels, join(): pl.pallas_call(join_kernel, grid=(N // STEP,), in_specs=[pl.BlockSpec((FR...  13 us
    all_to_all x1, starting transfers between devices, on_device(): lax.all_to_all(send, AXES, split_axis=0, concat_axis=0, tiled=True)  10.8 us
  transfers between devices with their start and end apart: 1, of which 1 were waited for; matrix products, arithmetic and copies ran while one was open for 0% of the time, Pallas kernels for 22%

profile of v2, /device:TPU:53, one launch (start us, length us, event | category | flops | bytes accessed | tf_op | source)
XLA Modules:
  0.0 149.9 jit_solution(10107633269572924632)
XLA Ops:
  0.6 20.1 %shard_map.41 = (f32[16512,128]{1,0:T(8,128)}, f32[4,128,128]{2,1,0:T(8,128)}, f32[4,32,128]{2,1,0:T(8,128)}) custom-call(f32[16384,128]{1,0:T(8,128)} %bitcast.3, f32[4,32]{1,0:T(4,128)} %b_ref.1), custom_call_target="tpu_custom_call" | custom-call | tf_op jit(solution)/shard_map/pallas_call | solution.py:131
  20.7 10.8 %all-to-all-start = ((f32[128,129,1,128]{3,2,1,0:T(1,128)}), f32[128,129,1,128]{3,2,1,0:T(1,128)}, u32[]{:S(2)}, u32[]{:S(2)}) async-start(f32[128,129,1,128]{3,2,1,0:T(1,128)} %bitcast.4), calls=%async_computation | async-start | bytes 16908288 | tf_op jit(solution)/shard_map/all_to_all | solution.py:303
  31.5 33.2 %shard_map.42.q_ref = f32[4,32,128,128]{3,2,1,0:T(8,128)} custom-call(f32[4,32,128,128]{3,2,1,0:T(8,128)} %c_ref.1, f32[4,128,128]{2,1,0:T(8,128)} %get-tuple-element.5.u_ref, f32[4,32,128]{2,1,0:T(8,128)} %get-tuple-element.6.v_ref), custom_call_target="tpu_custom_call" | custom-call | flops 8388608 | bytes 16777216 | tf_op jit(solution)/shard_map/pallas_call | solution.py:180
  64.7 72.2 %all-to-all-done = f32[128,129,1,128]{3,2,1,0:T(1,128)} async-done(((f32[128,129,1,128]{3,2,1,0:T(1,128)}), f32[128,129,1,128]{3,2,1,0:T(1,128)}, u32[]{:S(2)}, u32[]{:S(2)}) %all-to-all-start) | async-done | bytes 8454176 | tf_op jit(solution)/shard_map/all_to_all | solution.py:303
  136.9 13.0 %shard_map.43 = (f32[4,32,128,128]{3,2,1,0:T(8,128)}, f32[4,32]{1,0:T(4,128)}) custom-call(f32[4,32,128,128]{3,2,1,0:T(8,128)} %shard_map.42.q_ref, f32[16512,128]{1,0:T(8,128)} %bitcast.2.r_ref), custom_call_target="tpu_custom_call" | custom-call | tf_op jit(solution)/shard_map/pallas_call | solution.py:274
Async XLA Ops:
  20.7 116.2 %all-to-all-start = ((f32[128,129,1,128]{3,2,1,0:T(1,128)}), f32[128,129,1,128]{3,2,1,0:T(1,128)}, u32[]{:S(2)}, u32[]{:S(2)}) async-start(f32[128,129,1,128]{3,2,1,0:T(1,128)} %bitcast.4), calls=%async_computation | async-start | bytes 16908288 | tf_op jit(solution)/shard_map/all_to_all | solution.py:303

commit v3 on v2

--- a/solution.py
+++ b/solution.py
@@ -15,12 +15,16 @@
 leader_temper = 0.1
 LOG2E = 1.4426950408889634
 INNER = LOG2E / temper
-UNROLL = 8
+UNROLL = 32
 DEVICES = FAC * LOC
 PIECE = N + 1
-STEP = 16
+PITCH = N + 1
+PARTS = 2
+WIDTH = N // PARTS
+STEP = 32
 STEP_F = STEP // FR
-VMEM_LIMIT = 60 << 20
+SPACE = LR + 1
+VMEM_LIMIT = 67043328
 AXES = ("fac", "loc")
 
 
@@ -29,16 +33,33 @@
     return combine(x, pltpu.roll(x, 2 * LR, 1))
 
 
-def sweep_kernel(c_ref, b_ref, s_ref, u_ref, v_ref, d_ref, e_ref, m_ref, a_ref, w_ref, out_ref, line_ref, sem, line_sem):
+def sweep_kernel(c_ref, b_ref, s_ref, u_ref, v_ref, d_ref, e_ref, m_ref, a_ref, w_ref, in_ref, out_ref, line_ref, in_sem, sem, line_sem):
     slab = pl.program_id(0)
     slot = slab & 1
     loc = lax.axis_index("loc")
+
+    def fetch(at, to):
+        for part in range(PARTS):
+            for j in range(LR):
+                pltpu.make_async_copy(
+                    c_ref.at[pl.ds((at * LR + j) * N + part * WIDTH, WIDTH)],
+                    in_ref.at[to, pl.ds(j * PITCH + part * WIDTH, WIDTH)],
+                    in_sem.at[to, part],
+                ).start()
+
+    @pl.when(slab == 0)
+    def _():
+        fetch(0, 0)
+
+    @pl.when(slab + 1 < FR)
+    def _():
+        fetch(slab + 1, 1 - slot)
 
     def load(f, col_min):
         rows = []
         for g in range(LOC):
             k = (g + LOC - loc) & (LOC - 1)
-            rows.append(c_ref[pl.ds(FR * f + k, LR, stride=N), :])
+            rows.append(in_ref[slot, pl.ds(FR * f + k, LR, stride=PITCH), :])
         x = jnp.concatenate(rows, 0).T
         row_min = jnp.min(x, 0, keepdims=True)
         x = x - row_min
@@ -46,7 +67,12 @@
         m_ref[pl.ds(f, 1), :] = row_min
         return jnp.minimum(col_min, x)
 
-    col_min = lax.fori_loop(0, FAC, load, jnp.full((N, N), jnp.inf, jnp.float32), unroll=UNROLL)
+    col_min = jnp.full((N, N), jnp.inf, jnp.float32)
+    for part in range(PARTS):
+        pltpu.make_async_copy(
+            c_ref.at[pl.ds(0, LR * WIDTH)], in_ref.at[slot, pl.ds(0, LR * WIDTH)], in_sem.at[slot, part]
+        ).wait()
+        col_min = lax.fori_loop(part * WIDTH // FR, (part + 1) * WIDTH // FR, load, col_min, unroll=16)
     col_min = over_groups(col_min, jnp.minimum)
 
     weight = jnp.exp2(-INNER * col_min)
@@ -132,7 +158,7 @@
         sweep_kernel,
         grid=(FR,),
         in_specs=[
-            pl.BlockSpec((rows, N), lambda i: (i, 0)),
+            pl.BlockSpec(memory_space=pl.ANY),
             pl.BlockSpec((FR, LR), lambda i: (0, 0)),
         ],
         out_specs=[
@@ -151,8 +177,10 @@
             pltpu.VMEM((FAC, N), jnp.float32),
             pltpu.VMEM((FAC, N), jnp.float32),
             pltpu.VMEM((FR, N), jnp.float32),
+            pltpu.VMEM((2, LR * PITCH, N), jnp.float32),
             pltpu.VMEM((2, FAC * N, N), jnp.float32),
             pltpu.VMEM((1, N), jnp.float32),
+            pltpu.SemaphoreType.DMA((2, PARTS)),
             pltpu.SemaphoreType.DMA((2,)),
             pltpu.SemaphoreType.DMA,
         ],
@@ -217,10 +245,15 @@
 def join_kernel(q_ref, r_ref, o_ref, nb_ref, in_ref, lead_ref, bs_ref, sem, lead_sem):
     step = pl.program_id(0)
     slot = step & 1
-    sources = STEP_F * LOC
+    sources = STEP_F * LOC * FR
 
     def piece(at, n, to):
-        return pltpu.make_async_copy(r_ref.at[pl.ds((at * sources + n) * PIECE, N)], in_ref.at[to, n], sem.at[to, n])
+        f, g, i = n // (LOC * FR), n // FR % LOC, n % FR
+        return pltpu.make_async_copy(
+            r_ref.at[pl.ds(((at * STEP_F + f) * LOC + g) * PIECE + i * LR, LR)],
+            in_ref.at[to, g, pl.ds((f * FR + i) * SPACE, LR)],
+            sem.at[to],
+        )
 
     def fetch(at, to):
         for n in range(sources):
@@ -256,18 +289,12 @@
             row = pltpu.roll(row, (LOC - loc) * LR, 1)
             nb_ref[pl.ds(i, 1), :] = row[:, :LR]
 
-    for n in range(sources):
-        piece(step, n, slot).wait()
-    q_rows = q_ref.reshape(FR * LR * STEP, N)
-    o_rows = o_ref.reshape(FR * LR * STEP, N)
-    for g in range(STEP_F):
-        for k in range(FR):
-            for t in range(LR // 8):
-                parts = [in_ref[slot, g * LOC + s, pl.ds(k * LR + t * 8, 8), :] for s in range(LOC)]
-                parts = regroup(parts)
-                for a in range(FR):
-                    at = pl.ds((a * LR + t * 8) * STEP + g * FR + k, 8, stride=STEP)
-                    o_rows[at, :] = q_rows[at, :] + 0.5 * parts[a]
+    pltpu.make_async_copy(r_ref.at[pl.ds(0, sources * LR)], r_ref.at[pl.ds(0, sources * LR)], sem.at[slot]).wait()
+    for t in range(STEP // 8):
+        for b in range(LR):
+            parts = regroup([in_ref[slot, g, pl.ds(t * 8 * SPACE + b, 8, stride=SPACE), :] for g in range(LOC)])
+            for a in range(FR):
+                o_ref[a, b, pl.ds(t * 8, 8), :] = q_ref[a, b, pl.ds(t * 8, 8), :] + 0.5 * parts[a]
 
 
 def join(own, incoming):
@@ -287,10 +314,10 @@
             jax.ShapeDtypeStruct((FR, LR), jnp.float32),
         ],
         scratch_shapes=[
-            pltpu.VMEM((2, STEP_F * LOC, N, N), jnp.float32),
+            pltpu.VMEM((2, LOC, STEP * SPACE, N), jnp.float32),
             pltpu.VMEM((DEVICES, N), jnp.float32),
             pltpu.VMEM((N, N), jnp.float32),
-            pltpu.SemaphoreType.DMA((2, STEP_F * LOC)),
+            pltpu.SemaphoreType.DMA((2,)),
             pltpu.SemaphoreType.DMA,
         ],
         compiler_params=pltpu.CompilerParams(vmem_limit_bytes=VMEM_LIMIT),

time: 150 us -> 143 us (0.953)
  waiting for transfers between devices: 72.2 us -> 67 us
  Pallas kernels: 66.3 us -> 64 us
    pallas_call x1, Pallas kernels: 20.1 us -> 14.9 us  [sweeps(): pl.pallas_call(sweep_kernel, grid=(FR,), in_specs=[pl.BlockSpec(memory_sp...]
    all_to_all x1, waiting for transfers between devices: 72.2 us -> 67 us  [on_device(): lax.all_to_all(send, AXES, split_axis=0, concat_axis=0, tiled=True)]
    pallas_call x1, Pallas kernels: 33.2 us -> 38.4 us  [own_half(): pl.pallas_call(own_kernel, grid=(N // STEP,), in_specs=[pl.BlockSpec((FR,...]
    pallas_call x1, Pallas kernels: 13 us -> 10.7 us  [join(): pl.pallas_call(join_kernel, grid=(N // STEP,), in_specs=[pl.BlockSpec((FR...]
  transfers between devices with their start and end apart: 1 -> 1, of which waited for: 1 -> 1; matrix products, arithmetic and copies ran while one was open for 0% -> 0% of each run, Pallas kernels for 22% -> 27%
where the time goes in v3:
time: 143 us; the launch traced here: 142 us
  waiting for transfers between devices  67 us (47%)
  Pallas kernels  64 us (45%)
  starting transfers between devices  10.8 us (8%)
    all_to_all x1, waiting for transfers between devices, on_device(): lax.all_to_all(send, AXES, split_axis=0, concat_axis=0, tiled=True)  67 us
    pallas_call x1, Pallas kernels, own_half(): pl.pallas_call(own_kernel, grid=(N // STEP,), in_specs=[pl.BlockSpec((FR,...  38.4 us
    pallas_call x1, Pallas kernels, sweeps(): pl.pallas_call(sweep_kernel, grid=(FR,), in_specs=[pl.BlockSpec(memory_sp...  14.9 us
    all_to_all x1, starting transfers between devices, on_device(): lax.all_to_all(send, AXES, split_axis=0, concat_axis=0, tiled=True)  10.8 us
    pallas_call x1, Pallas kernels, join(): pl.pallas_call(join_kernel, grid=(N // STEP,), in_specs=[pl.BlockSpec((FR...  10.7 us
  transfers between devices with their start and end apart: 1, of which 1 were waited for; matrix products, arithmetic and copies ran while one was open for 0% of the time, Pallas kernels for 27%

profile of v3, /device:TPU:53, one launch (start us, length us, event | category | flops | bytes accessed | tf_op | source)
XLA Modules:
  0.0 142.4 jit_solution(15307750842008332357)
XLA Ops:
  0.6 14.9 %shard_map.41 = (f32[16512,128]{1,0:T(8,128)}, f32[4,128,128]{2,1,0:T(8,128)}, f32[4,32,128]{2,1,0:T(8,128)}) custom-call(f32[16384,128]{1,0:T(8,128)} %bitcast.3, f32[4,32]{1,0:T(4,128)} %b_ref.1), custom_call_target="tpu_custom_call" | custom-call | tf_op jit(solution)/shard_map/pallas_call | solution.py:157
  15.5 10.8 %all-to-all-start = ((f32[128,129,1,128]{3,2,1,0:T(1,128)}), f32[128,129,1,128]{3,2,1,0:T(1,128)}, u32[]{:S(2)}, u32[]{:S(2)}) async-start(f32[128,129,1,128]{3,2,1,0:T(1,128)} %bitcast.4), calls=%async_computation | async-start | bytes 16908288 | tf_op jit(solution)/shard_map/all_to_all | solution.py:330
  26.3 38.4 %shard_map.42.q_ref = f32[4,32,128,128]{3,2,1,0:T(8,128)} custom-call(f32[4,32,128,128]{3,2,1,0:T(8,128)} %c_ref.1, f32[4,128,128]{2,1,0:T(8,128)} %get-tuple-element.5.u_ref, f32[4,32,128]{2,1,0:T(8,128)} %get-tuple-element.6.v_ref), custom_call_target="tpu_custom_call" | custom-call | flops 8388608 | bytes 16777216 | tf_op jit(solution)/shard_map/pallas_call | solution.py:208
  64.7 67.0 %all-to-all-done = f32[128,129,1,128]{3,2,1,0:T(1,128)} async-done(((f32[128,129,1,128]{3,2,1,0:T(1,128)}), f32[128,129,1,128]{3,2,1,0:T(1,128)}, u32[]{:S(2)}, u32[]{:S(2)}) %all-to-all-start) | async-done | bytes 8454176 | tf_op jit(solution)/shard_map/all_to_all | solution.py:330
  131.7 10.7 %shard_map.43 = (f32[4,32,128,128]{3,2,1,0:T(8,128)}, f32[4,32]{1,0:T(4,128)}) custom-call(f32[4,32,128,128]{3,2,1,0:T(8,128)} %shard_map.42.q_ref, f32[16512,128]{1,0:T(8,128)} %bitcast.2.r_ref), custom_call_target="tpu_custom_call" | custom-call | tf_op jit(solution)/shard_map/pallas_call | solution.py:301
Async XLA Ops:
  15.5 116.2 %all-to-all-start = ((f32[128,129,1,128]{3,2,1,0:T(1,128)}), f32[128,129,1,128]{3,2,1,0:T(1,128)}, u32[]{:S(2)}, u32[]{:S(2)}) async-start(f32[128,129,1,128]{3,2,1,0:T(1,128)} %bitcast.4), calls=%async_computation | async-start | bytes 16908288 | tf_op jit(solution)/shard_map/all_to_all | solution.py:330

commit v4 on v3

--- a/solution.py
+++ b/solution.py
@@ -23,9 +23,10 @@
 WIDTH = N // PARTS
 STEP = 32
 STEP_F = STEP // FR
-SPACE = LR + 1
+BAND = 32
+SPACE = BAND + 1
 VMEM_LIMIT = 67043328
-AXES = ("fac", "loc")
+AXES = ("loc", "fac")
 
 
 def over_groups(x, combine):
@@ -111,7 +112,7 @@
         for s in range(LOC):
             pltpu.make_async_copy(
                 out_ref.at[slot, pl.ds(f * N + s * LR, LR)],
-                s_ref.at[pl.ds((f * LOC + s) * PIECE + slab * LR, LR)],
+                s_ref.at[pl.ds((s * FAC + f) * PIECE + slab * LR, LR)],
                 sem.at[slot],
             ).start()
 
@@ -127,7 +128,9 @@
     lax.fori_loop(0, FAC, emit, 0, unroll=UNROLL)
     ship(FAC - 1)
     row = m_ref[...] + row_part
-    u_ref[...] = jnp.concatenate([row, jnp.zeros((N - FAC, N), jnp.float32)], 0).T
+    for k in range(FR):
+        turn = ((LOC - k - loc) & (LOC - 1)) * LR
+        u_ref[pl.ds(k, FAC, stride=FR), :] = pltpu.roll(row, turn, 1)
     v_ref[...] = col.T[:LR]
     worth = over_groups(jnp.sum(row, 0, keepdims=True), jnp.add) + jnp.sum(col, 0, keepdims=True)
     w_ref[pl.ds(slab, 1), :] = worth * (1.0 / N)
@@ -186,38 +189,6 @@
         ],
         compiler_params=pltpu.CompilerParams(vmem_limit_bytes=VMEM_LIMIT),
     )(quad_cost.reshape(FR * rows, N), leader)
-
-
-def own_kernel(c_ref, u_ref, v_ref, o_ref):
-    step = pl.program_id(0)
-    loc = lax.axis_index("loc")
-    c_rows = c_ref.reshape(FR * LR * STEP, N)
-    o_rows = o_ref.reshape(FR * LR * STEP, N)
-    for g in range(STEP_F):
-        shift = lax.rem(N - (step * STEP_F + g), N)
-        for k in range(FR):
-            begin = ((k + loc) & (FR - 1)) * LR
-            for a in range(FR):
-                row = u_ref[a, pl.ds(pl.multiple_of(begin, LR), LR), :]
-                row = pltpu.roll(row, shift, 1)[:, :1]
-                at = pl.ds(a * LR * STEP + g * FR + k, LR, stride=STEP)
-                o_rows[at, :] = 0.5 * (c_rows[at, :] - row - v_ref[a])
-
-
-def own_half(quad_cost, row, col):
-    return pl.pallas_call(
-        own_kernel,
-        grid=(N // STEP,),
-        in_specs=[
-            pl.BlockSpec((FR, LR, STEP, N), lambda i: (0, 0, i, 0)),
-            pl.BlockSpec((FR, N, N), lambda i: (0, 0, 0)),
-            pl.BlockSpec((FR, LR, N), lambda i: (0, 0, 0)),
-        ],
-        out_specs=pl.BlockSpec((FR, LR, STEP, N), lambda i: (0, 0, i, 0)),
-        out_shape=jax.ShapeDtypeStruct((FR, LR, N, N), jnp.float32),
-        compiler_params=pltpu.CompilerParams(vmem_limit_bytes=VMEM_LIMIT),
-        cost_estimate=pl.CostEstimate(flops=1 << 23, bytes_accessed=1 << 24, transcendentals=0),
-    )(quad_cost, row, col)
 
 
 def regroup(parts):
@@ -242,29 +213,30 @@
     return -scale * (highest + jnp.log(totals))
 
 
-def join_kernel(q_ref, r_ref, o_ref, nb_ref, in_ref, lead_ref, bs_ref, sem, lead_sem):
-    step = pl.program_id(0)
+def join_kernel(c_ref, u_ref, v_ref, r_ref, o_ref, nb_ref, in_ref, lead_ref, bs_ref, sem, lead_sem):
+    at = pl.program_id(0)
+    band = pl.program_id(1)
+    bands = LR // BAND
+    step = at * bands + band
     slot = step & 1
-    sources = STEP_F * LOC * FR
-
-    def piece(at, n, to):
-        f, g, i = n // (LOC * FR), n // FR % LOC, n % FR
-        return pltpu.make_async_copy(
-            r_ref.at[pl.ds(((at * STEP_F + f) * LOC + g) * PIECE + i * LR, LR)],
-            in_ref.at[to, g, pl.ds((f * FR + i) * SPACE, LR)],
-            sem.at[to],
-        )
-
-    def fetch(at, to):
-        for n in range(sources):
-            piece(at, n, to).start()
+    pieces = STEP_F * LOC * FR
+
+    def fetch(at, band, to):
+        for f in range(STEP_F):
+            for g in range(LOC):
+                for i in range(FR):
+                    pltpu.make_async_copy(
+                        r_ref.at[pl.ds((g * FAC + at * STEP_F + f) * PIECE + i * LR + band * BAND, BAND)],
+                        in_ref.at[to, g, pl.ds((f * FR + i) * SPACE, BAND)],
+                        sem.at[to],
+                    ).start()
 
     def lead(d):
         return pltpu.make_async_copy(r_ref.at[pl.ds(d * PIECE + N, 1)], lead_ref.at[pl.ds(d, 1)], lead_sem)
 
     @pl.when(step == 0)
     def _():
-        fetch(0, 0)
+        fetch(0, 0, 0)
 
         def start(d, carry):
             lead(d).start()
@@ -272,15 +244,19 @@
 
         lax.fori_loop(0, DEVICES, start, 0, unroll=8)
 
-    @pl.when(step + 1 < pl.num_programs(0))
-    def _():
-        fetch(step + 1, 1 - slot)
+    @pl.when(step + 1 < pl.num_programs(0) * bands)
+    def _():
+        if bands == 1:
+            fetch(at + 1, 0, 1 - slot)
+        else:
+            wrap = band == bands - 1
+            fetch(jnp.where(wrap, at + 1, at), jnp.where(wrap, 0, band + 1), 1 - slot)
 
     @pl.when(step == 1)
     def _():
         pltpu.make_async_copy(r_ref.at[pl.ds(0, DEVICES)], lead_ref, lead_sem).wait()
-        fac, loc = (lax.axis_index(name) for name in AXES)
-        b = regroup([lead_ref[pl.ds(g, FAC, stride=LOC), :] for g in range(LOC)])
+        loc, fac = (lax.axis_index(name) for name in AXES)
+        b = regroup([lead_ref[pl.ds(g * FAC, FAC), :] for g in range(LOC)])
         b = [x - soft_min(x, 1, leader_temper) for x in b]
         b = jnp.concatenate(b, 0)
         bs_ref[...] = b - soft_min(b, 0, leader_temper)
@@ -289,25 +265,36 @@
             row = pltpu.roll(row, (LOC - loc) * LR, 1)
             nb_ref[pl.ds(i, 1), :] = row[:, :LR]
 
-    pltpu.make_async_copy(r_ref.at[pl.ds(0, sources * LR)], r_ref.at[pl.ds(0, sources * LR)], sem.at[slot]).wait()
+    pltpu.make_async_copy(r_ref.at[pl.ds(0, pieces * BAND)], r_ref.at[pl.ds(0, pieces * BAND)], sem.at[slot]).wait()
     for t in range(STEP // 8):
-        for b in range(LR):
+        rows = pl.ds(pl.multiple_of(at * STEP + t * 8, 8), 8)
+        for a in range(FR):
+            col = u_ref[a, rows, :]
+            if bands > 1:
+                col = pltpu.roll(col, (N - band * BAND) & (N - 1), 1)
+            if a == 0:
+                cols = []
+            cols.append(col)
+        for b in range(BAND):
             parts = regroup([in_ref[slot, g, pl.ds(t * 8 * SPACE + b, 8, stride=SPACE), :] for g in range(LOC)])
             for a in range(FR):
-                o_ref[a, b, pl.ds(t * 8, 8), :] = q_ref[a, b, pl.ds(t * 8, 8), :] + 0.5 * parts[a]
-
-
-def join(own, incoming):
+                own = c_ref[a, b, pl.ds(t * 8, 8), :] - cols[a][:, b : b + 1] - v_ref[a, pl.ds(b, 1), :]
+                o_ref[a, b, pl.ds(t * 8, 8), :] = 0.5 * (own + parts[a])
+
+
+def join(quad_cost, row, col, incoming):
     return pl.pallas_call(
         join_kernel,
-        grid=(N // STEP,),
+        grid=(N // STEP, LR // BAND),
         in_specs=[
-            pl.BlockSpec((FR, LR, STEP, N), lambda i: (0, 0, i, 0)),
+            pl.BlockSpec((FR, BAND, STEP, N), lambda i, b: (0, b, i, 0)),
+            pl.BlockSpec((FR, N, N), lambda i, b: (0, 0, 0)),
+            pl.BlockSpec((FR, BAND, N), lambda i, b: (0, b, 0)),
             pl.BlockSpec(memory_space=pl.ANY),
         ],
         out_specs=[
-            pl.BlockSpec((FR, LR, STEP, N), lambda i: (0, 0, i, 0)),
-            pl.BlockSpec((FR, LR), lambda i: (0, 0)),
+            pl.BlockSpec((FR, BAND, STEP, N), lambda i, b: (0, b, i, 0)),
+            pl.BlockSpec((FR, LR), lambda i, b: (0, 0)),
         ],
         out_shape=[
             jax.ShapeDtypeStruct((FR, LR, N, N), jnp.float32),
@@ -321,15 +308,14 @@
             pltpu.SemaphoreType.DMA,
         ],
         compiler_params=pltpu.CompilerParams(vmem_limit_bytes=VMEM_LIMIT),
-    )(own, incoming)
+    )(quad_cost, row, col, incoming)
 
 
 def on_device(quad_cost, leader):
     send, row, col = sweeps(quad_cost, leader)
     send = send.reshape(DEVICES, PIECE, 1, N)
     incoming = lax.all_to_all(send, AXES, split_axis=0, concat_axis=0, tiled=True)
-    own = own_half(quad_cost, row, col)
-    return tuple(join(own, incoming.reshape(DEVICES * PIECE, N)))
+    return tuple(join(quad_cost, row, col, incoming.reshape(DEVICES * PIECE, N)))
 
 
 def solution(mesh):

time: 143 us -> 139 us (0.972)
  the two profiles are of different devices: /device:TPU:53 before, /device:TPU:3 now
where the time goes in v4:
time: 139 us; the launch traced here: 138 us
  blocking collectives  111 us (80%)
  Pallas kernels  27.1 us (19%)
    all_to_all x1, blocking collectives, on_device(): lax.all_to_all(send, AXES, split_axis=0, concat_axis=0, tiled=True)  111 us
    pallas_call x1, Pallas kernels, sweeps(): pl.pallas_call(sweep_kernel, grid=(FR,), in_specs=[pl.BlockSpec(memory_sp...  14.9 us
    pallas_call x1, Pallas kernels, join(): pl.pallas_call(join_kernel, grid=(N // STEP, LR // BAND), in_specs=[pl.Bl...  12.2 us

profile of v4, /device:TPU:3, one launch (start us, length us, event | category | flops | bytes accessed | tf_op | source)
XLA Modules:
  0.0 138.3 jit_solution(857157065614641694)
XLA Ops:
  0.6 14.9 %shard_map.41 = (f32[16512,128]{1,0:T(8,128)}, f32[4,128,128]{2,1,0:T(8,128)}, f32[4,32,128]{2,1,0:T(8,128)}) custom-call(f32[16384,128]{1,0:T(8,128)} %bitcast.4, f32[4,32]{1,0:T(4,128)} %b_ref.1), custom_call_target="tpu_custom_call" | custom-call | tf_op jit(solution)/shard_map/pallas_call | solution.py:160
  15.5 110.6 %all_to_all.5 = f32[128,129,1,128]{3,2,1,0:T(1,128)} all-to-all(f32[128,129,1,128]{3,2,1,0:T(1,128)} %bitcast.5), channel_id=1, replica_groups=mesh['fac'=32,'loc'=4] {'loc','fac'}, dimensions={0} | all-to-all | bytes 16908288 | tf_op jit(solution)/shard_map/all_to_all | solution.py:317
  126.1 12.2 %shard_map.42 = (f32[4,32,128,128]{3,2,1,0:T(8,128)}, f32[4,32]{1,0:T(4,128)}) custom-call(f32[4,32,128,128]{3,2,1,0:T(8,128)} %c_ref.1, f32[4,128,128]{2,1,0:T(8,128)} %get-tuple-element.5.u_ref, f32[4,32,128]{2,1,0:T(8,128)} %get-tuple-element.6.v_ref, f32[16512,128]{1,0:T(8,128)} %bitcast.3), custom_call_target="tpu_custom_call" | custom-call | tf_op jit(solution)/shard_map/pallas_call | solution.py:286

commit v5 on v4

--- a/solution.py
+++ b/solution.py
@@ -26,6 +26,7 @@
 BAND = 32
 SPACE = BAND + 1
 VMEM_LIMIT = 67043328
+JOIN_LIMIT = 40 << 20
 AXES = ("loc", "fac")
 
 
@@ -278,7 +279,7 @@
         for b in range(BAND):
             parts = regroup([in_ref[slot, g, pl.ds(t * 8 * SPACE + b, 8, stride=SPACE), :] for g in range(LOC)])
             for a in range(FR):
-                own = c_ref[a, b, pl.ds(t * 8, 8), :] - cols[a][:, b : b + 1] - v_ref[a, pl.ds(b, 1), :]
+                own = c_ref[a, b, rows, :] - cols[a][:, b : b + 1] - v_ref[a, pl.ds(b, 1), :]
                 o_ref[a, b, pl.ds(t * 8, 8), :] = 0.5 * (own + parts[a])
 
 
@@ -287,7 +288,7 @@
         join_kernel,
         grid=(N // STEP, LR // BAND),
         in_specs=[
-            pl.BlockSpec((FR, BAND, STEP, N), lambda i, b: (0, b, i, 0)),
+            pl.BlockSpec(memory_space=pltpu.VMEM),
             pl.BlockSpec((FR, N, N), lambda i, b: (0, 0, 0)),
             pl.BlockSpec((FR, BAND, N), lambda i, b: (0, b, 0)),
             pl.BlockSpec(memory_space=pl.ANY),
@@ -307,7 +308,7 @@
             pltpu.SemaphoreType.DMA((2,)),
             pltpu.SemaphoreType.DMA,
         ],
-        compiler_params=pltpu.CompilerParams(vmem_limit_bytes=VMEM_LIMIT),
+        compiler_params=pltpu.CompilerParams(vmem_limit_bytes=JOIN_LIMIT),
     )(quad_cost, row, col, incoming)
 
 

time: 139 us -> 137 us (0.986)
  Pallas kernels: 27.1 us -> 24.7 us
    pallas_call x1, Pallas kernels: 12.2 us -> 9.76 us  [join(): pl.pallas_call(join_kernel, grid=(N // STEP, LR // BAND), in_specs=[pl.Bl...]
where the time goes in v5:
time: 137 us; the launch traced here: 136 us
  blocking collectives  111 us (81%)
  Pallas kernels  24.7 us (18%)
    all_to_all x1, blocking collectives, on_device(): lax.all_to_all(send, AXES, split_axis=0, concat_axis=0, tiled=True)  111 us
    pallas_call x1, Pallas kernels, sweeps(): pl.pallas_call(sweep_kernel, grid=(FR,), in_specs=[pl.BlockSpec(memory_sp...  14.9 us
    pallas_call x1, Pallas kernels, join(): pl.pallas_call(join_kernel, grid=(N // STEP, LR // BAND), in_specs=[pl.Bl...  9.76 us

profile of v5, /device:TPU:3, one launch (start us, length us, event | category | flops | bytes accessed | tf_op | source)
XLA Modules:
  0.0 135.9 jit_solution(15167080940306958412)
XLA Ops:
  0.6 14.9 %shard_map.41 = (f32[16512,128]{1,0:T(8,128)}, f32[4,128,128]{2,1,0:T(8,128)}, f32[4,32,128]{2,1,0:T(8,128)}) custom-call(f32[16384,128]{1,0:T(8,128)} %bitcast.3, f32[4,32]{1,0:T(4,128)} %b_ref.1), custom_call_target="tpu_custom_call" | custom-call | tf_op jit(solution)/shard_map/pallas_call | solution.py:161
  15.5 0.0 copy-start
  15.6 0.0 copy-start.1
  15.6 0.0 copy-start.2
  15.6 110.6 %all_to_all.5 = f32[128,129,1,128]{3,2,1,0:T(1,128)} all-to-all(f32[128,129,1,128]{3,2,1,0:T(1,128)} %bitcast.5), channel_id=1, replica_groups=mesh['fac'=32,'loc'=4] {'loc','fac'}, dimensions={0} | all-to-all | bytes 16908288 | tf_op jit(solution)/shard_map/all_to_all | solution.py:318
  126.2 0.0 copy-done
  126.2 0.0 copy-done.1
  126.2 0.0 copy-done.2
  126.2 9.8 %shard_map.42 = (f32[4,32,128,128]{3,2,1,0:T(8,128)}, f32[4,32]{1,0:T(4,128)}) custom-call(f32[4,32,128,128]{3,2,1,0:T(8,128)S(1)} %copy-done, f32[4,128,128]{2,1,0:T(8,128)S(1)} %copy-done.1, f32[4,32,128]{2,1,0:T(8,128)S(1)} %copy-done.2, f32[16512,128]{1,0:T(8,128)} %bitcast.4), custom_call_target="tpu_custom_call" | custom-call | tf_op jit(solution)/shard_map/pallas_call | solution.py:287
Async XLA Ops:
  15.5 110.6 %copy-start = (f32[4,32,128,128]{3,2,1,0:T(8,128)S(1)}, f32[4,32,128,128]{3,2,1,0:T(8,128)}, u32[]{:S(2)}) copy-start(f32[4,32,128,128]{3,2,1,0:T(8,128)} %c_ref.1) | copy-start | bytes 25165828
  15.6 110.6 %copy-start.1 = (f32[4,128,128]{2,1,0:T(8,128)S(1)}, f32[4,128,128]{2,1,0:T(8,128)}, u32[]{:S(2)}) copy-start(f32[4,128,128]{2,1,0:T(8,128)} %get-tuple-element.5.u_ref) | copy-start | bytes 786436
  15.6 110.6 %copy-start.2 = (f32[4,32,128]{2,1,0:T(8,128)S(1)}, f32[4,32,128]{2,1,0:T(8,128)}, u32[]{:S(2)}) copy-start(f32[4,32,128]{2,1,0:T(8,128)} %get-tuple-element.6.v_ref) | copy-start | bytes 196612

commit v6 on v5

--- a/solution.py
+++ b/solution.py
@@ -117,17 +117,6 @@
                 sem.at[slot],
             ).start()
 
-    def emit(f, carry):
-        out_ref[slot, pl.ds(pl.multiple_of(f * N, N), N), :] = d_ref[f] - col - a_ref[pl.ds(f, 1), :]
-
-        @pl.when(f > 0)
-        def _():
-            ship(f - 1)
-
-        return carry
-
-    lax.fori_loop(0, FAC, emit, 0, unroll=UNROLL)
-    ship(FAC - 1)
     row = m_ref[...] + row_part
     for k in range(FR):
         turn = ((LOC - k - loc) & (LOC - 1)) * LR
@@ -151,6 +140,21 @@
 
         lax.fori_loop(0, DEVICES, send, 0, unroll=8)
 
+
+    def emit(f, carry):
+        out_ref[slot, pl.ds(pl.multiple_of(f * N, N), N), :] = d_ref[f] - col - a_ref[pl.ds(f, 1), :]
+
+        @pl.when(f > 0)
+        def _():
+            ship(f - 1)
+
+        return carry
+
+    lax.fori_loop(0, FAC, emit, 0, unroll=UNROLL)
+    ship(FAC - 1)
+
+    @pl.when(slab == FR - 1)
+    def _():
         pltpu.make_async_copy(out_ref.at[0, pl.ds(0, DEVICES)], s_ref.at[pl.ds(0, DEVICES)], line_sem).wait()
         slab_done(1 - slot)
         slab_done(slot)

time: 137 us -> 137 us (level)
  no operation moved by 1% of the time
where the time goes in v6:
time: 137 us
  blocking collectives  111 us (81%)
  Pallas kernels  25.5 us (19%)
    all_to_all x1, blocking collectives, on_device(): lax.all_to_all(send, AXES, split_axis=0, concat_axis=0, tiled=True)  111 us
    pallas_call x1, Pallas kernels, sweeps(): pl.pallas_call(sweep_kernel, grid=(FR,), in_specs=[pl.BlockSpec(memory_sp...  15.8 us
    pallas_call x1, Pallas kernels, join(): pl.pallas_call(join_kernel, grid=(N // STEP, LR // BAND), in_specs=[pl.Bl...  9.76 us

profile of v6, /device:TPU:3, one launch (start us, length us, event | category | flops | bytes accessed | tf_op | source)
XLA Modules:
  0.0 136.8 jit_solution(13950303610179787310)
XLA Ops:
  0.6 15.8 %shard_map.41 = (f32[16512,128]{1,0:T(8,128)}, f32[4,128,128]{2,1,0:T(8,128)}, f32[4,32,128]{2,1,0:T(8,128)}) custom-call(f32[16384,128]{1,0:T(8,128)} %bitcast.3, f32[4,32]{1,0:T(4,128)} %b_ref.1), custom_call_target="tpu_custom_call" | custom-call | tf_op jit(solution)/shard_map/pallas_call | solution.py:165
  16.4 0.0 copy-start
  16.4 0.0 copy-start.1
  16.4 0.0 copy-start.2
  16.4 110.6 %all_to_all.5 = f32[128,129,1,128]{3,2,1,0:T(1,128)} all-to-all(f32[128,129,1,128]{3,2,1,0:T(1,128)} %bitcast.5), channel_id=1, replica_groups=mesh['fac'=32,'loc'=4] {'loc','fac'}, dimensions={0} | all-to-all | bytes 16908288 | tf_op jit(solution)/shard_map/all_to_all | solution.py:322
  127.0 0.0 copy-done
  127.0 0.0 copy-done.1
  127.0 0.0 copy-done.2
  127.0 9.8 %shard_map.42 = (f32[4,32,128,128]{3,2,1,0:T(8,128)}, f32[4,32]{1,0:T(4,128)}) custom-call(f32[4,32,128,128]{3,2,1,0:T(8,128)S(1)} %copy-done, f32[4,128,128]{2,1,0:T(8,128)S(1)} %copy-done.1, f32[4,32,128]{2,1,0:T(8,128)S(1)} %copy-done.2, f32[16512,128]{1,0:T(8,128)} %bitcast.4), custom_call_target="tpu_custom_call" | custom-call | tf_op jit(solution)/shard_map/pallas_call | solution.py:291
Async XLA Ops:
  16.4 110.6 %copy-start = (f32[4,32,128,128]{3,2,1,0:T(8,128)S(1)}, f32[4,32,128,128]{3,2,1,0:T(8,128)}, u32[]{:S(2)}) copy-start(f32[4,32,128,128]{3,2,1,0:T(8,128)} %c_ref.1) | copy-start | bytes 25165828
  16.4 110.6 %copy-start.1 = (f32[4,128,128]{2,1,0:T(8,128)S(1)}, f32[4,128,128]{2,1,0:T(8,128)}, u32[]{:S(2)}) copy-start(f32[4,128,128]{2,1,0:T(8,128)} %get-tuple-element.5.u_ref) | copy-start | bytes 786436
  16.4 110.6 %copy-start.2 = (f32[4,32,128]{2,1,0:T(8,128)S(1)}, f32[4,32,128]{2,1,0:T(8,128)}, u32[]{:S(2)}) copy-start(f32[4,32,128]{2,1,0:T(8,128)} %get-tuple-element.6.v_ref) | copy-start | bytes 196612
